TPU v7x, 256 devices: a whole 4x4x8 slice. The times are simulated.
256 devices in a mesh: lat: 4 (over z_lo), wave: 64 (over z_hi, y, x, core).
Axes of the slice: x: 4, y: 4, z: 8 (z_hi: 2, z_lo: 4; z = z_hi * 4 + z_lo), core: 2. Of those that a mesh axis runs over, the one named last changes fastest.
Arguments:
- fourier: bfloat16 [2, 1024, 1024, 128], P(None, ('lat', 'wave')), may hold values from -6 to 6
- cycle_points: int32 [1024], P(('lat', 'wave')), may hold values from 20 to 4120, as said below
- wave_table: int32 [1024], replicated, may hold values from 0 to 1023, as said below
- legendre: bfloat16 [1024, 1024, 1024], P('wave', 'lat'), as said below
Outputs:
- spectral: bfloat16 [1024, 1024, 128], P('wave', 'lat')
Inputs may be any that keep to these rules, and one draw needn't show every extreme that they name: wave_table is a permutation of 0 to 1023; slots 16 q to 16 q + 15 hold 16 consecutive wavenumbers in rising order. legendre[r, k, l] is zero wherever the degree wave_table[r] + 2 j + p exceeds 1024 - 1, with p = 1 if l >= 512 else 0 and j = l - p * 512. `cycle_points`: cycle k has about 4 k + 20 points.
All inputs are finite; a program needn't handle non-finite values.
Results may differ from a plain program's by a relative error of at most 0.0085.
Values may be sent and summed in bfloat16 or wider, within the bound.
No kernel may reach another device: no remote copies, remote signals or barrier semaphores. Data moves between devices by JAX's collectives and lax.ppermute only.
A program may use at most 128 MiB of HBM per device.

v0:
```python
import jax
import jax.numpy as jnp
from jax import lax
from jax.sharding import PartitionSpec as P


def contract(piece, inputs, bands):
    slots, cycles, columns = piece.shape
    cycle_band = cycles // bands
    left = piece.reshape(slots, bands, cycle_band, columns)
    right = inputs.reshape(bands, cycle_band, inputs.shape[1], inputs.shape[2])
    parts = jnp.einsum("mbkl,bkmc->bmlc", left, right, preferred_element_type=jnp.float32)
    return jnp.sum(parts.astype(jnp.bfloat16).astype(jnp.float32), axis=0)


def project(legendre, inputs, bands):
    return contract(legendre, inputs, bands)


def per_device(fourier, cycle_points, wave_table, legendre):
    waves_all = wave_table.shape[0]
    half = waves_all // 2
    waves = jnp.arange(waves_all, dtype=jnp.int32)
    present = (2 * waves[None, :] < cycle_points[:, None]).astype(jnp.bfloat16)
    kept = fourier * present[None, :, :, None]
    ordered = jnp.take(kept, wave_table, axis=2)
    banded = lax.all_to_all(ordered, "wave", split_axis=2, concat_axis=1, tiled=True)
    north = banded[0].astype(jnp.float32)
    south = banded[1].astype(jnp.float32)
    even_part = (north + south).astype(jnp.bfloat16)
    odd_part = (north - south).astype(jnp.bfloat16)
    moved = lax.all_to_all(legendre, "lat", split_axis=2, concat_axis=1, tiled=True)
    block_cols = moved.shape[2]
    first_col = lax.axis_index("lat") * block_cols
    parity = (first_col >= half).astype(jnp.int32)
    even_all, odd_all = (
        lax.all_gather(even_part, "lat", axis=0, tiled=True),
        lax.all_gather(odd_part, "lat", axis=0, tiled=True),
    )
    gathered = jnp.where(parity == 1, odd_all, even_all)
    result = project(moved, gathered, lax.axis_size("lat"))
    return result.astype(jnp.bfloat16)


def solution(mesh):
    placed = (P(None, ("lat", "wave"), None, None), P(("lat", "wave")), P(), P("wave", "lat", None))
    return jax.shard_map(
        per_device, mesh=mesh, in_specs=placed, out_specs=P("wave", "lat", None), check_vma=False
    )
```

profile of v0, /device:TPU:1, one launch (start us, length us, event | category | flops | bytes accessed | tf_op | source)
XLA Modules:
  0.0 455.1 jit_solution(8741149732136601205)
XLA Ops:
  6.5 0.0 all-gather.3.cloned.1.call-start
  6.5 0.7 fusion.9
  7.2 0.7 compare_and_fusion
  7.9 0.7 compare_convert_fusion
  8.7 0.2 copy.17
  8.9 4.6 %copy_multiply_fusion = bf16[2,4,1024,128]{3,1,2,0:T(4,128)(2,1)} fusion(bf16[2,4,1024,128]{3,2,1,0:T(8,128)(2,1)} %param.4, bf16[4,1024]{0,1:T(8,128)(2,1)S(1)} %copy.17), kind=kLoop, calls=%fused_computation.11 | loop fusion | flops 1048576 | bytes 4202496 | tf_op jit(solution)/shard_map/mul | solution.py:25
  13.4 6.0 %gather_fusion = bf16[1024,2,4,128]{3,2,1,0:T(4,128)(2,1)S(1)} fusion(bf16[2,4,1024,128]{3,1,2,0:T(4,128)(2,1)} %copy_multiply_fusion, s32[1024]{0:T(1024)S(1)} %fusion.9), kind=kCustom, calls=%fused_computation | custom fusion | bytes 4198400 | tf_op jit(solution)/shard_map/jit(_take)/gather | solution.py:26
  19.5 3.8 select_bitcast_fusion
  23.3 53.2 %all_to_all.30 = bf16[2,4,1024,128]{3,1,0,2:T(4,128)(2,1)S(1)} all-to-all(bf16[2,4,1024,128]{3,1,0,2:T(4,128)(2,1)S(1)} %select_bitcast_fusion), channel_id=1, replica_groups=mesh['lat'=4,'wave'=64] {'wave'}, dimensions={2} | all-to-all | bytes 4194304 | tf_op jit(solution)/shard_map/all_to_all | solution.py:27
  76.5 0.6 copy.33
  77.2 1.9 fusion.8
  79.1 0.0 all-gather.3.cloned.1.call-update
  79.1 12.6 %copy.20 = bf16[16,256,1024]{1,0,2:T(8,128)(2,1)} copy(bf16[16,256,1024]{2,1,0:T(8,128)(2,1)} %param.7) | data formatting | bytes 16777216 | tf_op args[3]
  91.7 18.9 %all-to-all-start.1 = ((bf16[16,256,1024]{1,0,2:T(8,128)(2,1)}), bf16[16,256,1024]{1,0,2:T(8,128)(2,1)}, u32[]{:S(2)}, u32[]{:S(2)}) async-start(bf16[16,256,1024]{1,0,2:T(8,128)(2,1)} %copy.20), calls=%async_computation.1 | async-start | bytes 16777216 | tf_op jit(solution)/shard_map/all_to_all | solution.py:32
  110.6 0.0 all-gather.5.cloned.1.call-start
  110.6 0.7 all-gather.5.cloned.1.call-update
  111.3 136.6 %all-gather.3.cloned.1.call-done = bf16[1024,16,128]{2,1,0:T(8,128)(2,1)} async-done(((bf16[256,16,128]{2,1,0:T(8,128)(2,1)}), bf16[1024,16,128]{2,1,0:T(8,128)(2,1)}) %all-gather.3.cloned.1.call-update) | async-done | bytes 4194320 | tf_op jit(solution)/shard_map/all_gather | solution.py:38
  247.9 174.3 %all-gather.5.cloned.1.call-done = bf16[1024,16,128]{2,1,0:T(8,128)(2,1)} async-done(((bf16[256,16,128]{2,1,0:T(8,128)(2,1)}), bf16[1024,16,128]{2,1,0:T(8,128)(2,1)}) %all-gather.5.cloned.1.call-update) | async-done | bytes 4194320 | tf_op jit(solution)/shard_map/all_gather | solution.py:37
  422.2 4.6 %broadcast_select_fusion = bf16[1024,16,128]{2,1,0:T(8,128)(2,1)} fusion(bf16[1024,16,128]{2,1,0:T(8,128)(2,1)} %all-gather.3.cloned.1.call-done, bf16[1024,16,128]{2,1,0:T(8,128)(2,1)} %all-gather.5.cloned.1.call-done, pred[]{:T(512)S(6)} %eq.3), kind=kLoop, calls=%fused_computation.5 | loop fusion | flops 2097152 | bytes 12582913 | tf_op jit(solution)/shard_map/jit(_where)/select_n | solution.py:40
  426.8 0.0 all-to-all-done.1
  426.8 13.8 %copy.22 = bf16[16,256,4,256]{3,1,0,2:T(8,128)(2,1)} copy(bf16[16,256,4,256]{1,0,3,2:T(8,128)(2,1)} %bitcast.6) | data formatting | bytes 16777216 | tf_op jit(solution)/shard_map/all_to_all | solution.py:32
  440.6 6.3 %convert_reduce_fusion = bf16[16,128,256]{2,1,0:T(8,128)(2,1)S(1)} fusion(bf16[16,256,4,256]{3,1,0,2:T(8,128)(2,1)} %copy.22, bf16[4,256,16,128]{3,2,1,0:T(8,128)(2,1)} %bitcast.18), kind=kOutput, calls=%fused_computation.4 | convolution fusion | flops 1077411840 | bytes 13631488 | tf_op jit(solution)/shard_map/mbkl,bkmc->bmlc/dot_general | solution.py:12
  446.9 1.3 copy.24
  (1 shorter events, 0.0 us)
Async XLA Ops:
  6.5 241.4 %all-gather.3.cloned.1.call-start = ((), (), s32[]{:S(2)}) async-start(), calls=%async_computation.2 | async-start | bytes 5242880 | tf_op jit(solution)/shard_map/all_gather | solution.py:38
  91.7 335.1 %all-to-all-start.1 = ((bf16[16,256,1024]{1,0,2:T(8,128)(2,1)}), bf16[16,256,1024]{1,0,2:T(8,128)(2,1)}, u32[]{:S(2)}, u32[]{:S(2)}) async-start(bf16[16,256,1024]{1,0,2:T(8,128)(2,1)} %copy.20), calls=%async_computation.1 | async-start | bytes 16777216 | tf_op jit(solution)/shard_map/all_to_all | solution.py:32
  110.6 311.6 %all-gather.5.cloned.1.call-start = ((), (), s32[]{:S(2)}) async-start(), calls=%async_computation.3 | async-start | bytes 5242880 | tf_op jit(solution)/shard_map/all_gather | solution.py:37
Sparse Core Ops, SparseCore 0:
  79.2 168.6 all-gather.2
  249.7 172.4 all-gather.4
where the time goes:
time: 456 us; the launch traced here: 455 us
  waiting for transfers between devices  312 us (68%)
  blocking collectives  53.2 us (12%)
  local copies, waits for them, and re-layouts  34.6 us (8%)
  starting transfers between devices  18.9 us (4%)
  other arithmetic  17 us (4%)
  between operations  13.4 us (3%)
  matrix products  6.34 us (1%)
    all_gather x1, waiting for transfers between devices, per_device(): lax.all_gather(even_part, 'lat', axis=0, tiled=True)  174 us
    all_gather x1, waiting for transfers between devices, per_device(): lax.all_gather(odd_part, 'lat', axis=0, tiled=True)  137 us
    all_to_all x1, blocking collectives, per_device(): lax.all_to_all(ordered, 'wave', split_axis=2, concat_axis=1, tiled=True)  53.2 us
    all_to_all x1, starting transfers between devices, per_device(): lax.all_to_all(legendre, 'lat', split_axis=2, concat_axis=1, tiled=True)  18.9 us
    all_to_all x1, local copies, waits for them, and re-layouts, per_device(): lax.all_to_all(legendre, 'lat', split_axis=2, concat_axis=1, tiled=True)  13.8 us
    unnamed x1, local copies, waits for them, and re-layouts  12.6 us
  transfers between devices with their start and end apart: 3, of which 2 were waited for; matrix products, arithmetic and copies ran while one was open for 4% of the time, Pallas kernels for 0%

commit v1 on v0

--- a/solution.py
+++ b/solution.py
@@ -34,7 +34,9 @@
     first_col = lax.axis_index("lat") * block_cols
     parity = (first_col >= half).astype(jnp.int32)
     even_all, odd_all = (
-        lax.all_gather(even_part, "lat", axis=0, tiled=True),
+        jnp.concatenate(
+            lax.all_to_all(jnp.stack([even_part] * lax.axis_size("lat")), "lat", 0, 0), axis=0
+        ),
         lax.all_gather(odd_part, "lat", axis=0, tiled=True),
     )
     gathered = jnp.where(parity == 1, odd_all, even_all)

time: 456 us -> 479 us (1.050)
  waiting for transfers between devices: 312 us -> 328 us
  starting transfers between devices: 18.9 us -> 24.3 us
    all_gather x1 -> x0, waiting for transfers between devices: 174 us -> none  [per_device(): lax.all_gather(even_part, 'lat', axis=0, tiled=True)]
    all_to_all x1, waiting for transfers between devices: 0.01 us -> 94.3 us  [per_device(): lax.all_to_all(legendre, 'lat', split_axis=2, concat_axis=1, tiled=True)]
    all_to_all x0 -> x1, waiting for transfers between devices: none -> 82.1 us  [per_device(): lax.all_to_all(jnp.stack([even_part] * lax.axis_size('lat')), 'lat', 0, 0)]
    all_to_all x0 -> x1, starting transfers between devices: none -> 18.6 us  [per_device(): lax.all_to_all(jnp.stack([even_part] * lax.axis_size('lat')), 'lat', 0, 0)]
    all_gather x1, waiting for transfers between devices: 137 us -> 151 us  [per_device(): lax.all_gather(odd_part, 'lat', axis=0, tiled=True)]
    all_to_all x1, starting transfers between devices: 18.9 us -> 5.64 us  [per_device(): lax.all_to_all(legendre, 'lat', split_axis=2, concat_axis=1, tiled=True)]
  transfers between devices with their start and end apart: 3 -> 3, of which waited for: 2 -> 3; matrix products, arithmetic and copies ran while one was open for 4% -> 4% of each run, Pallas kernels for 0% -> 0%
where the time goes in v1:
time: 479 us; the launch traced here: 478 us
  waiting for transfers between devices  328 us (68%)
  blocking collectives  53.2 us (11%)
  local copies, waits for them, and re-layouts  37 us (8%)
  starting transfers between devices  24.3 us (5%)
  other arithmetic  16.5 us (3%)
  between operations  13.5 us (3%)
  matrix products  6.34 us (1%)
    all_gather x1, waiting for transfers between devices, per_device(): lax.all_gather(odd_part, 'lat', axis=0, tiled=True)  151 us
    all_to_all x1, waiting for transfers between devices, per_device(): lax.all_to_all(legendre, 'lat', split_axis=2, concat_axis=1, tiled=True)  94.3 us
    all_to_all x1, waiting for transfers between devices, per_device(): lax.all_to_all(jnp.stack([even_part] * lax.axis_size('lat')), 'lat', 0, 0)  82.1 us
    all_to_all x1, blocking collectives, per_device(): lax.all_to_all(ordered, 'wave', split_axis=2, concat_axis=1, tiled=True)  53.2 us
    all_to_all x1, starting transfers between devices, per_device(): lax.all_to_all(jnp.stack([even_part] * lax.axis_size('lat')), 'lat', 0, 0)  18.6 us
    all_to_all x1, local copies, waits for them, and re-layouts, per_device(): lax.all_to_all(legendre, 'lat', split_axis=2, concat_axis=1, tiled=True)  13.7 us
    unnamed x1, local copies, waits for them, and re-layouts  12.6 us
  transfers between devices with their start and end apart: 3, of which 3 were waited for; matrix products, arithmetic and copies ran while one was open for 4% of the time, Pallas kernels for 0%

profile of v1, /device:TPU:1, one launch (start us, length us, event | category | flops | bytes accessed | tf_op | source)
XLA Modules:
  0.0 478.4 jit_solution(2572070027382079758)
XLA Ops:
  6.5 0.7 compare_and_fusion
  7.2 0.7 fusion.9
  7.9 0.7 compare_convert_fusion
  8.7 0.2 copy.17
  8.9 4.6 copy_multiply_fusion
  13.4 6.0 %gather_fusion = bf16[1024,2,4,128]{3,2,1,0:T(4,128)(2,1)S(1)} fusion(bf16[2,4,1024,128]{3,1,2,0:T(4,128)(2,1)} %copy_multiply_fusion, s32[1024]{0:T(1024)S(1)} %fusion.9), kind=kCustom, calls=%fused_computation | custom fusion | bytes 4198400 | tf_op jit(solution)/shard_map/jit(_take)/gather | solution.py:26
  19.4 3.8 select_bitcast_fusion
  23.3 53.2 %all_to_all.35 = bf16[2,4,1024,128]{3,1,0,2:T(4,128)(2,1)S(1)} all-to-all(bf16[2,4,1024,128]{3,1,0,2:T(4,128)(2,1)S(1)} %select_bitcast_fusion), channel_id=1, replica_groups=mesh['lat'=4,'wave'=64] {'wave'}, dimensions={2} | all-to-all | bytes 4194304 | tf_op jit(solution)/shard_map/all_to_all | solution.py:27
  76.5 0.6 copy.33
  77.2 1.4 fusion.8
  78.6 2.5 stack.2
  81.0 18.6 %all-to-all-start.1 = ((bf16[4,256,16,128]{3,2,1,0:T(8,128)(2,1)}), bf16[4,256,16,128]{3,2,1,0:T(8,128)(2,1)}, u32[]{:S(2)}, u32[]{:S(2)}) async-start(bf16[4,256,16,128]{3,2,1,0:T(8,128)(2,1)} %stack.2), calls=%async_computation.1 | async-start | bytes 8388608 | tf_op jit(solution)/shard_map/all_to_all | solution.py:38
  99.6 12.6 %copy.20 = bf16[16,256,1024]{1,0,2:T(8,128)(2,1)} copy(bf16[16,256,1024]{2,1,0:T(8,128)(2,1)} %param.7) | data formatting | bytes 16777216 | tf_op args[3]
  112.2 82.1 %all-to-all-done.1 = bf16[4,256,16,128]{3,2,1,0:T(8,128)(2,1)} async-done(((bf16[4,256,16,128]{3,2,1,0:T(8,128)(2,1)}), bf16[4,256,16,128]{3,2,1,0:T(8,128)(2,1)}, u32[]{:S(2)}, u32[]{:S(2)}) %all-to-all-start.1) | async-done | bytes 4194336 | tf_op jit(solution)/shard_map/all_to_all | solution.py:38
  194.3 5.6 %all-to-all-start.2 = ((bf16[16,256,1024]{1,0,2:T(8,128)(2,1)}), bf16[16,256,1024]{1,0,2:T(8,128)(2,1)}, u32[]{:S(2)}, u32[]{:S(2)}) async-start(bf16[16,256,1024]{1,0,2:T(8,128)(2,1)} %copy.20), calls=%async_computation.2 | async-start | bytes 16777216 | tf_op jit(solution)/shard_map/all_to_all | solution.py:32
  199.9 0.0 all-gather.2.cloned.1.call-start
  200.0 0.7 all-gather.2.cloned.1.call-update
  200.7 150.5 %all-gather.2.cloned.1.call-done = bf16[1024,16,128]{2,1,0:T(8,128)(2,1)} async-done(((bf16[256,16,128]{2,1,0:T(8,128)(2,1)}), bf16[1024,16,128]{2,1,0:T(8,128)(2,1)}) %all-gather.2.cloned.1.call-update) | async-done | bytes 4194320 | tf_op jit(solution)/shard_map/all_gather | solution.py:40
  351.2 4.6 bitcast_select_fusion
  355.8 94.3 %all-to-all-done.2 = bf16[16,256,1024]{1,0,2:T(8,128)(2,1)} async-done(((bf16[16,256,1024]{1,0,2:T(8,128)(2,1)}), bf16[16,256,1024]{1,0,2:T(8,128)(2,1)}, u32[]{:S(2)}, u32[]{:S(2)}) %all-to-all-start.2) | async-done | bytes 8388640 | tf_op jit(solution)/shard_map/all_to_all | solution.py:32
  450.1 13.7 %copy.22 = bf16[16,256,4,256]{3,1,0,2:T(8,128)(2,1)} copy(bf16[16,256,4,256]{1,0,3,2:T(8,128)(2,1)} %bitcast.7) | data formatting | bytes 16777216 | tf_op jit(solution)/shard_map/all_to_all | solution.py:32
  463.9 6.3 %convert_reduce_fusion = bf16[16,128,256]{2,1,0:T(8,128)(2,1)S(1)} fusion(bf16[16,256,4,256]{3,1,0,2:T(8,128)(2,1)} %copy.22, bf16[4,256,16,128]{3,2,1,0:T(8,128)(2,1)} %bitcast.20), kind=kOutput, calls=%fused_computation.5 | convolution fusion | flops 1077411840 | bytes 13631488 | tf_op jit(solution)/shard_map/mbkl,bkmc->bmlc/dot_general | solution.py:12
  470.2 1.3 copy.24
  (1 shorter events, 0.0 us)
Async XLA Ops:
  81.0 113.3 %all-to-all-start.1 = ((bf16[4,256,16,128]{3,2,1,0:T(8,128)(2,1)}), bf16[4,256,16,128]{3,2,1,0:T(8,128)(2,1)}, u32[]{:S(2)}, u32[]{:S(2)}) async-start(bf16[4,256,16,128]{3,2,1,0:T(8,128)(2,1)} %stack.2), calls=%async_computation.1 | async-start | bytes 8388608 | tf_op jit(solution)/shard_map/all_to_all | solution.py:38
  194.3 255.8 %all-to-all-start.2 = ((bf16[16,256,1024]{1,0,2:T(8,128)(2,1)}), bf16[16,256,1024]{1,0,2:T(8,128)(2,1)}, u32[]{:S(2)}, u32[]{:S(2)}) async-start(bf16[16,256,1024]{1,0,2:T(8,128)(2,1)} %copy.20), calls=%async_computation.2 | async-start | bytes 16777216 | tf_op jit(solution)/shard_map/all_to_all | solution.py:32
  199.9 151.3 %all-gather.2.cloned.1.call-start = ((), (), s32[]{:S(2)}) async-start(), calls=%async_computation.3 | async-start | bytes 5242880 | tf_op jit(solution)/shard_map/all_gather | solution.py:40
Sparse Core Ops, SparseCore 0:
  202.6 148.5 all-gather.1
